TPU v7x, 32 devices: a whole 2x2x4 slice. The times are simulated.
32 devices in a mesh: layer: 2 (over core), tok: 16 (over z, y, x).
Axes of the slice: x: 2, y: 2, z: 4, core: 2. Of those that a mesh axis runs over, the one named last changes fastest.
Arguments:
- train_act: bfloat16 [4, 32768, 256], P('layer', 'tok'), may hold values from -0.75 to 0.75
- train_grad: bfloat16 [4, 32768, 256], P('layer', 'tok'), may hold values from -0.75 to 0.75
- test_act: bfloat16 [4, 2048, 256], P('layer', 'tok'), may hold values from -0.75 to 0.75
- test_grad: bfloat16 [4, 2048, 256], P('layer', 'tok'), may hold values from -0.75 to 0.75
- segment_ids: int32 [2048], replicated, may hold values from 0 to 127, as said below
Outputs:
- scores: float32 [128, 32768], P('layer', 'tok')
Inputs may be any that keep to these rules, and one draw needn't show every extreme that they name: `segment_ids`: each of the 128 queries has exactly 16 test tokens, placed anywhere among the 2048.
All inputs are finite; a program needn't handle non-finite values.
Results may differ from a plain program's by a relative error of at most 0.0029.
Values may be sent and summed in bfloat16 or wider, within the bound.
A program may use at most 128 MiB of HBM per device.

v0:
```python
import math

import jax
import jax.numpy as jnp
from jax import lax
from jax.sharding import PartitionSpec as P

Q = 128


def gram_product(test_a, test_g, train_a, train_g):
    act_gram = jnp.einsum("sp,tp->st", test_a, train_a, preferred_element_type=jnp.float32)
    grad_gram = jnp.einsum("sp,tp->st", test_g, train_g, preferred_element_type=jnp.float32)
    return (act_gram * grad_gram).astype(jnp.bfloat16)


def on_device(train_act, train_grad, test_act, test_grad, segment_ids):
    layer_count = train_act.shape[0]
    train_rows = train_act.shape[1]
    labels = jnp.arange(Q, dtype=jnp.int32)[:, None]
    empty = jnp.zeros((Q, train_rows), jnp.float32)
    running = empty
    act_rows = lax.all_gather(test_act, "tok", axis=1, tiled=True)
    grad_rows = lax.all_gather(test_grad, "tok", axis=1, tiled=True)
    for layer_idx in range(layer_count):
        add_running = running
        add_act_rows = act_rows[layer_idx]
        add_grad_rows = grad_rows[layer_idx]
        row_count = add_act_rows.shape[0]
        stride = math.gcd(row_count, 512)
        for offset in range(0, row_count, stride):
            query_of = lax.dynamic_slice_in_dim(segment_ids, offset, stride)
            select = (query_of[None, :] == labels).astype(jnp.bfloat16)
            product = gram_product(
                add_act_rows[offset : offset + stride],
                add_grad_rows[offset : offset + stride],
                train_act[layer_idx],
                train_grad[layer_idx],
            )
            add_running = add_running + jnp.dot(select, product, preferred_element_type=jnp.float32)
        running = add_running
    return lax.psum_scatter(running, "layer", scatter_dimension=0, tiled=True)


def solution(mesh):
    placed = (
        P("layer", "tok", None),
        P("layer", "tok", None),
        P("layer", "tok", None),
        P("layer", "tok", None),
        P(),
    )
    return jax.shard_map(
        on_device, mesh=mesh, in_specs=placed, out_specs=P("layer", "tok"), check_vma=False
    )
```

profile of v0, /device:TPU:0, one launch (start us, length us, event | category | flops | bytes accessed | tf_op | source)
XLA Modules:
  0.0 180.7 jit_solution(1979498510128110999)
XLA Ops:
  6.5 0.0 all-gather.3.cloned.1.call-start
  6.5 0.7 all-gather.3.cloned.1.call-update
  7.3 0.0 all-gather.5.cloned.1.call-start
  7.3 0.7 all-gather.5.cloned.1.call-update
  8.0 0.0 reduce-scatter.2.cloned.1.call-start
  8.1 0.8 fusion.65
  8.8 0.0 copy-start
  8.8 64.4 %all-gather.3.cloned.1.call-done = bf16[2,2048,256]{2,1,0:T(8,128)(2,1)} async-done(((bf16[2,128,256]{2,1,0:T(8,128)(2,1)}), bf16[2,2048,256]{2,1,0:T(8,128)(2,1)}) %all-gather.3.cloned.1.call-update) | async-done | bytes 2097168 | tf_op jit(solution)/shard_map/all_gather | solution.py:23
  73.2 0.0 copy-start.2
  73.2 4.2 %fusion.31 = f32[512,2048]{1,0:T(8,128)} fusion(bf16[2,2048,256]{2,1,0:T(8,128)(2,1)} %param.5, bf16[2,2048,256]{2,1,0:T(8,128)(2,1)} %all-gather.3.cloned.1.call-done), kind=kOutput, calls=%fused_computation.38 | convolution fusion | flops 536870912 | bytes 5505024 | tf_op jit(solution)/shard_map/sp,tp->st/dot_general | solution.py:12
  77.3 0.0 copy-done
  77.3 0.0 copy-done.2
  77.4 2.7 %fusion.29 = f32[512,2048]{1,0:T(8,128)} fusion(bf16[2,2048,256]{2,1,0:T(8,128)(2,1)S(1)} %copy-done, bf16[2,2048,256]{2,1,0:T(8,128)(2,1)S(1)} %copy-done.2), kind=kOutput, calls=%fused_computation.36 | convolution fusion | flops 536870912 | bytes 5505024 | tf_op jit(solution)/shard_map/sp,tp->st/dot_general | solution.py:12
  80.1 2.7 %fusion.27 = f32[512,2048]{1,0:T(8,128)} fusion(bf16[2,2048,256]{2,1,0:T(8,128)(2,1)S(1)} %copy-done, bf16[2,2048,256]{2,1,0:T(8,128)(2,1)S(1)} %copy-done.2), kind=kOutput, calls=%fused_computation.34 | convolution fusion | flops 536870912 | bytes 5505024 | tf_op jit(solution)/shard_map/sp,tp->st/dot_general | solution.py:12
  82.7 2.7 %fusion.25 = f32[512,2048]{1,0:T(8,128)} fusion(bf16[2,2048,256]{2,1,0:T(8,128)(2,1)S(1)} %copy-done, bf16[2,2048,256]{2,1,0:T(8,128)(2,1)S(1)} %copy-done.2), kind=kOutput, calls=%fused_computation.32 | convolution fusion | flops 536870912 | bytes 5505024 | tf_op jit(solution)/shard_map/sp,tp->st/dot_general | solution.py:12
  85.4 2.7 %fusion.15 = f32[512,2048]{1,0:T(8,128)} fusion(bf16[2,2048,256]{2,1,0:T(8,128)(2,1)S(1)} %copy-done, bf16[2,2048,256]{2,1,0:T(8,128)(2,1)S(1)} %copy-done.2), kind=kOutput, calls=%fused_computation.26 | convolution fusion | flops 536870912 | bytes 5505024 | tf_op jit(solution)/shard_map/sp,tp->st/dot_general | solution.py:12
  88.1 2.7 %fusion.13 = f32[512,2048]{1,0:T(8,128)} fusion(bf16[2,2048,256]{2,1,0:T(8,128)(2,1)S(1)} %copy-done, bf16[2,2048,256]{2,1,0:T(8,128)(2,1)S(1)} %copy-done.2), kind=kOutput, calls=%fused_computation.24 | convolution fusion | flops 536870912 | bytes 5505024 | tf_op jit(solution)/shard_map/sp,tp->st/dot_general | solution.py:12
  90.8 2.7 %fusion.11 = f32[512,2048]{1,0:T(8,128)} fusion(bf16[2,2048,256]{2,1,0:T(8,128)(2,1)S(1)} %copy-done, bf16[2,2048,256]{2,1,0:T(8,128)(2,1)S(1)} %copy-done.2), kind=kOutput, calls=%fused_computation.22 | convolution fusion | flops 536870912 | bytes 5505024 | tf_op jit(solution)/shard_map/sp,tp->st/dot_general | solution.py:12
  93.5 2.7 %fusion.9 = f32[512,2048]{1,0:T(8,128)} fusion(bf16[2,2048,256]{2,1,0:T(8,128)(2,1)S(1)} %copy-done, bf16[2,2048,256]{2,1,0:T(8,128)(2,1)S(1)} %copy-done.2), kind=kOutput, calls=%fused_computation.20 | convolution fusion | flops 536870912 | bytes 5505024 | tf_op jit(solution)/shard_map/sp,tp->st/dot_general | solution.py:12
  96.2 38.8 %all-gather.5.cloned.1.call-done = bf16[2,2048,256]{2,1,0:T(8,128)(2,1)} async-done(((bf16[2,128,256]{2,1,0:T(8,128)(2,1)}), bf16[2,2048,256]{2,1,0:T(8,128)(2,1)}) %all-gather.5.cloned.1.call-update) | async-done | bytes 2097168 | tf_op jit(solution)/shard_map/all_gather | solution.py:24
  135.0 0.0 copy-start.1
  135.0 3.8 %fusion = f32[128,2048]{1,0:T(8,128)S(1)} fusion(f32[512,2048]{1,0:T(8,128)} %fusion.31, bf16[2,2048,256]{2,1,0:T(8,128)(2,1)} %param.6, bf16[2,2048,256]{2,1,0:T(8,128)(2,1)} %all-gather.5.cloned.1.call-done, s32[512]{0:T(512)S(1)} %get-tuple-element.7), kind=kOutput, calls=%fused_computation.15 | convolution fusion | flops 807469056 | bytes 6555648 | tf_op jit(solution)/shard_map/dot_general | solution.py:40
  138.8 0.0 copy-done.1
  138.8 4.3 %convolution_add_fusion.6 = f32[128,2048]{1,0:T(8,128)} fusion(f32[128,2048]{1,0:T(8,128)S(1)} %fusion, f32[512,2048]{1,0:T(8,128)} %fusion.29, bf16[2,2048,256]{2,1,0:T(8,128)(2,1)S(1)} %copy-done.1, bf16[2,2048,256]{2,1,0:T(8,128)(2,1)} %all-gather.5.cloned.1.call-done, s32[512]{0:T(512)S(1)} %get-tuple-element.6), kind=kOutput, calls=%fused_computation.14 | convolution fusion | flops 807731200 | bytes 7604224 | tf_op jit(solution)/shard_map/dot_general | solution.py:40
  143.1 3.6 %convolution_add_fusion.5 = f32[128,2048]{1,0:T(8,128)S(1)} fusion(f32[128,2048]{1,0:T(8,128)} %convolution_add_fusion.6, f32[512,2048]{1,0:T(8,128)} %fusion.27, bf16[2,2048,256]{2,1,0:T(8,128)(2,1)S(1)} %copy-done.1, bf16[2,2048,256]{2,1,0:T(8,128)(2,1)} %all-gather.5.cloned.1.call-done, s32[512]{0:T(512)S(1)} %get-tuple-element.8), kind=kOutput, calls=%fused_computation.13 | convolution fusion | flops 807731200 | bytes 7604224 | tf_op jit(solution)/shard_map/dot_general | solution.py:40
  146.7 4.3 %convolution_add_fusion.4 = f32[128,2048]{1,0:T(8,128)} fusion(f32[128,2048]{1,0:T(8,128)S(1)} %convolution_add_fusion.5, f32[512,2048]{1,0:T(8,128)} %fusion.25, bf16[2,2048,256]{2,1,0:T(8,128)(2,1)S(1)} %copy-done.1, bf16[2,2048,256]{2,1,0:T(8,128)(2,1)} %all-gather.5.cloned.1.call-done, s32[512]{0:T(512)S(1)} %get-tuple-element.5), kind=kOutput, calls=%fused_computation.12 | convolution fusion | flops 807731200 | bytes 7604224 | tf_op jit(solution)/shard_map/dot_general | solution.py:40
  151.0 3.6 %convolution_add_fusion.3 = f32[128,2048]{1,0:T(8,128)S(1)} fusion(f32[128,2048]{1,0:T(8,128)} %convolution_add_fusion.4, f32[512,2048]{1,0:T(8,128)} %fusion.15, bf16[2,2048,256]{2,1,0:T(8,128)(2,1)S(1)} %copy-done.1, bf16[2,2048,256]{2,1,0:T(8,128)(2,1)} %all-gather.5.cloned.1.call-done, s32[512]{0:T(512)S(1)} %get-tuple-element.7), kind=kOutput, calls=%fused_computation.11 | convolution fusion | flops 807731200 | bytes 7604224 | tf_op jit(solution)/shard_map/dot_general | solution.py:40
  154.6 4.4 %convolution_add_fusion.2 = f32[128,2048]{1,0:T(8,128)} fusion(f32[128,2048]{1,0:T(8,128)S(1)} %convolution_add_fusion.3, f32[512,2048]{1,0:T(8,128)} %fusion.13, bf16[2,2048,256]{2,1,0:T(8,128)(2,1)S(1)} %copy-done.1, bf16[2,2048,256]{2,1,0:T(8,128)(2,1)} %all-gather.5.cloned.1.call-done, s32[512]{0:T(512)S(1)} %get-tuple-element.6), kind=kOutput, calls=%fused_computation.10 | convolution fusion | flops 807731200 | bytes 7604224 | tf_op jit(solution)/shard_map/dot_general | solution.py:40
  159.0 3.6 %convolution_add_fusion.1 = f32[128,2048]{1,0:T(8,128)S(1)} fusion(f32[128,2048]{1,0:T(8,128)} %convolution_add_fusion.2, f32[512,2048]{1,0:T(8,128)} %fusion.11, bf16[2,2048,256]{2,1,0:T(8,128)(2,1)S(1)} %copy-done.1, bf16[2,2048,256]{2,1,0:T(8,128)(2,1)} %all-gather.5.cloned.1.call-done, s32[512]{0:T(512)S(1)} %get-tuple-element.8), kind=kOutput, calls=%fused_computation.9 | convolution fusion | flops 807731200 | bytes 7604224 | tf_op jit(solution)/shard_map/dot_general | solution.py:40
  162.6 4.3 %convolution_add_fusion = f32[128,2048]{1,0:T(8,128)} fusion(f32[128,2048]{1,0:T(8,128)S(1)} %convolution_add_fusion.1, f32[512,2048]{1,0:T(8,128)} %fusion.9, bf16[2,2048,256]{2,1,0:T(8,128)(2,1)S(1)} %copy-done.1, bf16[2,2048,256]{2,1,0:T(8,128)(2,1)} %all-gather.5.cloned.1.call-done, s32[512]{0:T(512)S(1)} %get-tuple-element.5), kind=kOutput, calls=%fused_computation.8 | convolution fusion | flops 807731200 | bytes 7604224 | tf_op jit(solution)/shard_map/dot_general | solution.py:40
  166.9 0.0 reduce-scatter.2.cloned.1.call-update
  166.9 7.3 %reduce-scatter.2.cloned.1.call-done = f32[64,2048]{1,0:T(8,128)} async-done(((f32[128,2048]{1,0:T(8,128)}), f32[64,2048]{1,0:T(8,128)}) %reduce-scatter.2.cloned.1.call-update) | async-done | bytes 524304 | tf_op jit(solution)/shard_map/reduce_scatter | solution.py:42
Async XLA Ops:
  6.5 66.6 %all-gather.3.cloned.1.call-start = ((), (), s32[]{:S(2)}) async-start(), calls=%async_computation.1 | async-start | bytes 2228224 | tf_op jit(solution)/shard_map/all_gather | solution.py:23
  7.3 127.8 %all-gather.5.cloned.1.call-start = ((), (), s32[]{:S(2)}) async-start(), calls=%async_computation.2 | async-start | bytes 2228224 | tf_op jit(solution)/shard_map/all_gather | solution.py:24
  8.0 166.1 %reduce-scatter.2.cloned.1.call-start = ((), (), s32[]{:S(2)}) async-start(), calls=%async_computation.3 | async-start | bytes 1572864 | tf_op jit(solution)/shard_map/reduce_scatter | solution.py:42
  8.8 68.5 %copy-start = (bf16[2,2048,256]{2,1,0:T(8,128)(2,1)S(1)}, bf16[2,2048,256]{2,1,0:T(8,128)(2,1)}, u32[]{:S(2)}) copy-start(bf16[2,2048,256]{2,1,0:T(8,128)(2,1)} %param.5) | copy-start | bytes 6291460
  73.2 4.2 %copy-start.2 = (bf16[2,2048,256]{2,1,0:T(8,128)(2,1)S(1)}, bf16[2,2048,256]{2,1,0:T(8,128)(2,1)}, u32[]{:S(2)}) copy-start(bf16[2,2048,256]{2,1,0:T(8,128)(2,1)} %all-gather.3.cloned.1.call-done) | copy-start | bytes 6291460
  135.0 3.8 %copy-start.1 = (bf16[2,2048,256]{2,1,0:T(8,128)(2,1)S(1)}, bf16[2,2048,256]{2,1,0:T(8,128)(2,1)}, u32[]{:S(2)}) copy-start(bf16[2,2048,256]{2,1,0:T(8,128)(2,1)} %param.6) | copy-start | bytes 6291460
Sparse Core Ops, SparseCore 0:
  10.1 63.0 all-gather.2
  75.9 59.0 all-gather.4
  167.0 7.0 reduce-scatter.1
where the time goes:
time: 181 us
  waiting for transfers between devices  112 us (62%)
  matrix products  54.8 us (30%)
  between operations  13.2 us (7%)
    all_gather x1, waiting for transfers between devices, on_device(): act_rows = lax.all_gather(test_act, 'tok', axis=1, tiled=True)  64.4 us
    all_gather x1, waiting for transfers between devices, on_device(): grad_rows = lax.all_gather(test_grad, 'tok', axis=1, tiled=True)  38.8 us
    dot_general x8, matrix products, on_device(): jnp.dot(select, product, preferred_element_type=jnp.float32)  31.8 us
    dot_general x8, matrix products, gram_product(): jnp.einsum('sp,tp->st', test_a, train_a, preferred_element_type=jnp.float32)  23 us
    reduce_scatter x1, waiting for transfers between devices, on_device(): return lax.psum_scatter(running, 'layer', scatter_dimension=0, tiled=True)  7.26 us
  transfers between devices with their start and end apart: 3, of which 3 were waited for; matrix products, arithmetic and copies ran while one was open for 13% of the time, Pallas kernels for 0%

commit v1 on v0

v1 whole, which is shorter than its diff:
```python
import functools
import math

import jax
import jax.numpy as jnp
from jax import lax
from jax.experimental import pallas as pl
from jax.experimental.pallas import tpu as pltpu
from jax.sharding import PartitionSpec as P

Q = 128
MESH = pl.DeviceIdType.MESH


def kernel(
    layers,
    line,
    train_a,
    train_g,
    test_a,
    test_g,
    ids_ref,
    out_ref,
    ta,
    tg,
    buf,
    acc,
    xbuf,
    train_sem,
    own_sem,
    recv_sem,
    send_sem,
    xs_sem,
    xr_sem,
):
    me = lax.axis_index("tok")
    core = lax.axis_index("layer")
    z = me // 4
    y = (me // 2) % 2
    x = me % 2
    own_col = y * 2 + x
    x_col = y * 2 + (1 - x)
    y_col = (1 - y) * 2 + x
    d_col = (1 - y) * 2 + (1 - x)
    x_dev = z * 4 + x_col
    y_dev = z * 4 + y_col
    has_up = z < line - 1
    has_down = z > 0
    layer_count, train_rows, _ = ta.shape
    rows = buf.shape[3]
    q_block = Q // layers

    for which, (src, dst) in enumerate(((train_a, ta), (train_g, tg))):
        pltpu.make_async_copy(src, dst, train_sem.at[which]).start()
    for which, src in enumerate((test_a, test_g)):
        pltpu.make_async_copy(src, buf.at[which, me], own_sem.at[which]).start()

    barrier = pltpu.get_barrier_semaphore()

    def greet(where):
        pl.semaphore_signal(barrier, inc=1, device_id=where, device_id_type=MESH)

    greet({"tok": x_dev})
    greet({"tok": y_dev})
    pl.when(has_up)(lambda: greet({"tok": me + 4}))
    pl.when(has_down)(lambda: greet({"tok": me - 4}))
    for step in range(1, layers):
        greet({"layer": lax.rem(core + step, layers)})
    ends = jnp.where(has_up, 1, 0) + jnp.where(has_down, 1, 0)
    pl.semaphore_wait(barrier, layers + 1 + ends)

    def copy(route, which, zz, peer, to, src=None):
        return pltpu.make_async_remote_copy(
            src_ref=buf.at[which, peer] if src is None else src,
            dst_ref=buf.at[which, peer],
            send_sem=send_sem.at[route, which, zz],
            recv_sem=recv_sem.at[which, peer],
            device_id={"tok": to},
            device_id_type=MESH,
        )

    def arrived(which, peer):
        copy(0, which, 0, peer, x_dev).wait_recv()

    def nth(i):
        low = z < line - 1 - z
        near = jnp.where(low, z, line - 1 - z)
        half = (i + 1) // 2
        side = jnp.where(i % 2 == 1, z - half, z + half)
        rest = jnp.where(low, i, line - 1 - i)
        return jnp.where(i <= 2 * near, side, rest)

    for which, src in enumerate((test_a, test_g)):
        pl.when(has_up)(lambda: copy(3, which, z, me, me + 4, src).start())
        pl.when(has_down)(lambda: copy(4, which, z, me, me - 4, src).start())
        copy(0, which, z, me, x_dev, src).start()
        copy(1, which, z, me, y_dev, src).start()

    acc[...] = jnp.zeros_like(acc)
    tile = math.gcd(train_rows, 512)
    labels = lax.broadcasted_iota(jnp.int32, (Q, rows), 0)
    nt = (((1,), (1,)), ((), ()))

    def accumulate(peer):
        select = jnp.where(ids_ref[peer] == labels, 1.0, 0.0).astype(jnp.bfloat16)

        def one_tile(j, carry):
            at = pl.ds(pl.multiple_of(j * tile, tile), tile)
            product = None
            for layer in range(layer_count):
                a_gram = lax.dot_general(
                    buf[0, peer, layer], ta[layer, at, :], nt, preferred_element_type=jnp.float32
                )
                g_gram = lax.dot_general(
                    buf[1, peer, layer], tg[layer, at, :], nt, preferred_element_type=jnp.float32
                )
                term = a_gram * g_gram
                product = term if product is None else product + term
            acc[:, at] += jnp.dot(
                select, product.astype(jnp.bfloat16), preferred_element_type=jnp.float32
            )
            return carry

        lax.fori_loop(0, train_rows // tile, one_tile, 0)

    for which, (src, dst) in enumerate(((train_a, ta), (train_g, tg))):
        pltpu.make_async_copy(src, dst, train_sem.at[which]).wait()
    for which, src in enumerate((test_a, test_g)):
        pltpu.make_async_copy(src, buf.at[which, me], own_sem.at[which]).wait()

    def stage(i, carry):
        zi = nth(i)

        @pl.when(i < line)
        def _():
            accumulate(zi * 4 + own_col)

        @pl.when(i + 1 < line)
        def _():
            zn = nth(i + 1)
            peer = zn * 4 + own_col
            for which in range(2):
                arrived(which, peer)
                pl.when((zn < z) & has_up)(lambda: copy(3, which, zn, peer, me + 4).start())
                pl.when((zn > z) & has_down)(lambda: copy(4, which, zn, peer, me - 4).start())
                copy(0, which, zn, peer, x_dev).start()
                copy(1, which, zn, peer, y_dev).start()

        @pl.when(i < line)
        def _():
            from_x = zi * 4 + x_col
            from_y = zi * 4 + y_col
            arrived(0, from_x)
            copy(2, 0, zi, from_x, y_dev).start()
            arrived(0, from_y)
            arrived(1, from_y)
            copy(2, 1, zi, from_y, x_dev).start()
            arrived(1, from_x)

            def both(k, c):
                accumulate(jnp.where(k == 0, from_x, from_y))
                return c

            lax.fori_loop(0, 2, both, 0)

        @pl.when(i > 0)
        def _():
            peer = nth(i - 1) * 4 + d_col
            arrived(0, peer)
            arrived(1, peer)
            accumulate(peer)

        return carry

    lax.fori_loop(0, line + 1, stage, 0)

    def exchange(step):
        to = lax.rem(core + step, layers)
        return pltpu.make_async_remote_copy(
            src_ref=acc.at[pl.ds(pl.multiple_of(to * q_block, q_block), q_block)],
            dst_ref=xbuf.at[step - 1],
            send_sem=xs_sem.at[step - 1],
            recv_sem=xr_sem.at[step - 1],
            device_id={"layer": to},
            device_id_type=MESH,
        )

    for step in range(1, layers):
        exchange(step).start()

    def drain(zz, carry):
        for which in range(2):
            peer = zz * 4 + own_col
            copy(0, which, zz, peer, x_dev).wait_send()
            copy(1, which, zz, peer, y_dev).wait_send()
            copy(2, which, zz, peer, y_dev).wait_send()
            pl.when((zz <= z) & has_up)(lambda: copy(3, which, zz, peer, me + 4).wait_send())
            pl.when((zz >= z) & has_down)(lambda: copy(4, which, zz, peer, me - 4).wait_send())
        return carry

    lax.fori_loop(0, line, drain, 0)

    mine = pl.ds(pl.multiple_of(core * q_block, q_block), q_block)
    for step in range(1, layers):
        exchange(step).wait_recv()
    result = acc[mine, :]
    for step in range(1, layers):
        result = result + xbuf[step - 1]
    out_ref[...] = result
    for step in range(1, layers):
        exchange(step).wait_send()


def on_device(layers, toks, train_act, train_grad, test_act, test_grad, segment_ids):
    layer_count, train_rows, width = train_act.shape
    rows = test_act.shape[1]
    line = toks // 4
    q_block = Q // layers
    ids = segment_ids.reshape(toks, 1, rows)
    dma = pltpu.SemaphoreType.DMA
    anywhere = pl.BlockSpec(memory_space=pl.ANY)
    return pl.pallas_call(
        functools.partial(kernel, layers, line),
        out_shape=jax.ShapeDtypeStruct((q_block, train_rows), jnp.float32),
        in_specs=[anywhere] * 4 + [pl.BlockSpec(memory_space=pltpu.VMEM)],
        out_specs=pl.BlockSpec(memory_space=pltpu.VMEM),
        scratch_shapes=[
            pltpu.VMEM((layer_count, train_rows, width), jnp.bfloat16),
            pltpu.VMEM((layer_count, train_rows, width), jnp.bfloat16),
            pltpu.VMEM((2, toks, layer_count, rows, width), jnp.bfloat16),
            pltpu.VMEM((Q, train_rows), jnp.float32),
            pltpu.VMEM((layers - 1, q_block, train_rows), jnp.float32),
            dma((2,)),
            dma((2,)),
            dma((2, toks)),
            dma((5, 2, line)),
            dma((layers - 1,)),
            dma((layers - 1,)),
        ],
        compiler_params=pltpu.CompilerParams(
            collective_id=0, has_side_effects=True, vmem_limit_bytes=63 * 1024 * 1024
        ),
    )(train_act, train_grad, test_act, test_grad, ids)


def solution(mesh):
    placed = (
        P("layer", "tok", None),
        P("layer", "tok", None),
        P("layer", "tok", None),
        P("layer", "tok", None),
        P(),
    )
    body = functools.partial(on_device, mesh.shape["layer"], mesh.shape["tok"])
    return jax.shard_map(
        body, mesh=mesh, in_specs=placed, out_specs=P("layer", "tok"), check_vma=False
    )
```

time: 181 us -> 62.6 us (0.35)
  waiting for transfers between devices: 112 us -> 0 us
  Pallas kernels: 0 us -> 60.5 us
  matrix products: 54.8 us -> 0 us
  between operations: 13.2 us -> 0.01 us
    all_gather x2 -> x0, waiting for transfers between devices: 103 us -> none  [the longest x1 64.4 us: on_device(): act_rows = lax.all_gather(test_act, 'tok', axis=1, tiled=True)]
    pallas_call x0 -> x1, Pallas kernels: none -> 60.5 us  [on_device(): pl.pallas_call(functools.partial(kernel, layers, line), out_shape=jax.Sha...]
    dot_general x16 -> x0, matrix products: 54.8 us -> none  [the longest x8 31.8 us: on_device(): jnp.dot(select, product, preferred_element_type=jnp.float32)]
    reduce_scatter x1 -> x0, waiting for transfers between devices: 7.26 us -> none  [on_device(): return lax.psum_scatter(running, 'layer', scatter_dimension=0, tiled=True)]
    unnamed x6 -> x1, local copies, waits for them, and re-layouts: 0.01 us -> 1.87 us
  transfers between devices with their start and end apart: 3 -> 0, of which waited for: 3 -> 0; matrix products, arithmetic and copies ran while one was open for 13% -> 0% of each run, Pallas kernels for 0% -> 0%
where the time goes in v1:
time: 62.6 us; the launch traced here: 62.4 us
  Pallas kernels  60.5 us (97%)
  local copies, waits for them, and re-layouts  1.87 us (3%)
    pallas_call x1, Pallas kernels, on_device(): pl.pallas_call(functools.partial(kernel, layers, line), out_shape=jax.Sha...  60.5 us
    unnamed x1, local copies, waits for them, and re-layouts  1.87 us

profile of v1, /device:TPU:0, one launch (start us, length us, event | category | flops | bytes accessed | tf_op | source)
XLA Modules:
  0.0 62.4 jit_solution(4378373643419211794)
XLA Ops:
  0.0 60.5 %shard_map.55 = f32[64,2048]{1,0:T(8,128)} custom-call(bf16[2,2048,256]{2,1,0:T(8,128)(2,1)} %train_a.1, bf16[2,2048,256]{2,1,0:T(8,128)(2,1)} %train_g.1, bf16[2,128,256]{2,1,0:T(8,128)(2,1)} %test_a.1, bf16[2,128,256]{2,1,0:T(8,128)(2,1)} %test_g.1, s32[16,1,128]{2,1,0:T(1,128)} %bitcast.1), custom_call_target="tpu_custom_call" | custom-call | tf_op jit(solution)/shard_map/pallas_call | solution.py:222
  60.5 1.9 %copy.7 = f32[64,2048]{1,0:T(8,128)} copy(f32[64,2048]{1,0:T(8,128)} %shard_map.55) | data formatting | bytes 1048576

commit v2 on v1

--- a/solution.py
+++ b/solution.py
@@ -53,7 +53,7 @@
     for which, (src, dst) in enumerate(((train_a, ta), (train_g, tg))):
         pltpu.make_async_copy(src, dst, train_sem.at[which]).start()
     for which, src in enumerate((test_a, test_g)):
-        pltpu.make_async_copy(src, buf.at[which, me], own_sem.at[which]).start()
+        pltpu.make_async_copy(src, buf.at[which, :, z * 4], own_sem.at[which]).start()
 
     barrier = pltpu.get_barrier_semaphore()
 
@@ -69,18 +69,18 @@
     ends = jnp.where(has_up, 1, 0) + jnp.where(has_down, 1, 0)
     pl.semaphore_wait(barrier, layers + 1 + ends)
 
-    def copy(route, which, zz, peer, to, src=None):
+    def copy(route, which, zz, held, there, to, src=None):
         return pltpu.make_async_remote_copy(
-            src_ref=buf.at[which, peer] if src is None else src,
-            dst_ref=buf.at[which, peer],
+            src_ref=buf.at[which, :, zz * 4 + held] if src is None else src,
+            dst_ref=buf.at[which, :, zz * 4 + there],
             send_sem=send_sem.at[route, which, zz],
-            recv_sem=recv_sem.at[which, peer],
+            recv_sem=recv_sem.at[which, zz * 4 + there],
             device_id={"tok": to},
             device_id_type=MESH,
         )
 
-    def arrived(which, peer):
-        copy(0, which, 0, peer, x_dev).wait_recv()
+    def arrived(which, zz, there):
+        copy(0, which, zz, 0, there, x_dev).wait_recv()
 
     def nth(i):
         low = z < line - 1 - z
@@ -91,33 +91,40 @@
         return jnp.where(i <= 2 * near, side, rest)
 
     for which, src in enumerate((test_a, test_g)):
-        pl.when(has_up)(lambda: copy(3, which, z, me, me + 4, src).start())
-        pl.when(has_down)(lambda: copy(4, which, z, me, me - 4, src).start())
-        copy(0, which, z, me, x_dev, src).start()
-        copy(1, which, z, me, y_dev, src).start()
+        pl.when(has_up)(lambda: copy(3, which, z, 0, 0, me + 4, src).start())
+        pl.when(has_down)(lambda: copy(4, which, z, 0, 0, me - 4, src).start())
+        copy(0, which, z, 0, 2, x_dev, src).start()
+        copy(1, which, z, 0, 3, y_dev, src).start()
 
     acc[...] = jnp.zeros_like(acc)
-    tile = math.gcd(train_rows, 512)
+    tile = math.gcd(train_rows, 1024)
     labels = lax.broadcasted_iota(jnp.int32, (Q, rows), 0)
     nt = (((1,), (1,)), ((), ()))
 
-    def accumulate(peer):
-        select = jnp.where(ids_ref[peer] == labels, 1.0, 0.0).astype(jnp.bfloat16)
+    def accumulate(zz, first, columns):
+        one_hot = [
+            jnp.where(ids_ref[zz * 4 + c] == labels, 1.0, 0.0).astype(jnp.bfloat16)
+            for c in columns
+        ]
+        select = jnp.concatenate(one_hot * layer_count, axis=1)
+        pair = pl.ds(zz * 4 + first, 2)
+
+        def held(which, layer):
+            return buf[which, layer, pair].reshape(2 * rows, buf.shape[4])
 
         def one_tile(j, carry):
             at = pl.ds(pl.multiple_of(j * tile, tile), tile)
-            product = None
+            products = []
             for layer in range(layer_count):
                 a_gram = lax.dot_general(
-                    buf[0, peer, layer], ta[layer, at, :], nt, preferred_element_type=jnp.float32
+                    held(0, layer), ta[layer, at, :], nt, preferred_element_type=jnp.float32
                 )
                 g_gram = lax.dot_general(
-                    buf[1, peer, layer], tg[layer, at, :], nt, preferred_element_type=jnp.float32
+                    held(1, layer), tg[layer, at, :], nt, preferred_element_type=jnp.float32
                 )
-                term = a_gram * g_gram
-                product = term if product is None else product + term
+                products.append((a_gram * g_gram).astype(jnp.bfloat16))
             acc[:, at] += jnp.dot(
-                select, product.astype(jnp.bfloat16), preferred_element_type=jnp.float32
+                select, jnp.concatenate(products, axis=0), preferred_element_type=jnp.float32
             )
             return carry
 
@@ -126,49 +133,37 @@
     for which, (src, dst) in enumerate(((train_a, ta), (train_g, tg))):
         pltpu.make_async_copy(src, dst, train_sem.at[which]).wait()
     for which, src in enumerate((test_a, test_g)):
-        pltpu.make_async_copy(src, buf.at[which, me], own_sem.at[which]).wait()
+        pltpu.make_async_copy(src, buf.at[which, :, z * 4], own_sem.at[which]).wait()
 
     def stage(i, carry):
         zi = nth(i)
-
-        @pl.when(i < line)
-        def _():
-            accumulate(zi * 4 + own_col)
 
         @pl.when(i + 1 < line)
         def _():
             zn = nth(i + 1)
-            peer = zn * 4 + own_col
             for which in range(2):
-                arrived(which, peer)
-                pl.when((zn < z) & has_up)(lambda: copy(3, which, zn, peer, me + 4).start())
-                pl.when((zn > z) & has_down)(lambda: copy(4, which, zn, peer, me - 4).start())
-                copy(0, which, zn, peer, x_dev).start()
-                copy(1, which, zn, peer, y_dev).start()
+                arrived(which, zn, 0)
+                pl.when((zn < z) & has_up)(lambda: copy(3, which, zn, 0, 0, me + 4).start())
+                pl.when((zn > z) & has_down)(lambda: copy(4, which, zn, 0, 0, me - 4).start())
+                copy(0, which, zn, 0, 2, x_dev).start()
+                copy(1, which, zn, 0, 3, y_dev).start()
 
         @pl.when(i < line)
         def _():
-            from_x = zi * 4 + x_col
-            from_y = zi * 4 + y_col
-            arrived(0, from_x)
-            copy(2, 0, zi, from_x, y_dev).start()
-            arrived(0, from_y)
-            arrived(1, from_y)
-            copy(2, 1, zi, from_y, x_dev).start()
-            arrived(1, from_x)
-
-            def both(k, c):
-                accumulate(jnp.where(k == 0, from_x, from_y))
-                return c
-
-            lax.fori_loop(0, 2, both, 0)
+            arrived(0, zi, 2)
+            copy(2, 0, zi, 2, 1, y_dev).start()
+            arrived(0, zi, 3)
+            arrived(1, zi, 3)
+            copy(2, 1, zi, 3, 1, x_dev).start()
+            arrived(1, zi, 2)
+            accumulate(zi, 2, (x_col, y_col))
 
         @pl.when(i > 0)
         def _():
-            peer = nth(i - 1) * 4 + d_col
-            arrived(0, peer)
-            arrived(1, peer)
-            accumulate(peer)
+            zd = nth(i - 1)
+            for which in range(2):
+                arrived(which, zd, 1)
+            accumulate(zd, 0, (own_col, d_col))
 
         return carry
 
@@ -190,12 +185,11 @@
 
     def drain(zz, carry):
         for which in range(2):
-            peer = zz * 4 + own_col
-            copy(0, which, zz, peer, x_dev).wait_send()
-            copy(1, which, zz, peer, y_dev).wait_send()
-            copy(2, which, zz, peer, y_dev).wait_send()
-            pl.when((zz <= z) & has_up)(lambda: copy(3, which, zz, peer, me + 4).wait_send())
-            pl.when((zz >= z) & has_down)(lambda: copy(4, which, zz, peer, me - 4).wait_send())
+            copy(0, which, zz, 0, 2, x_dev).wait_send()
+            copy(1, which, zz, 0, 3, y_dev).wait_send()
+            copy(2, which, zz, 2, 1, y_dev).wait_send()
+            pl.when((zz <= z) & has_up)(lambda: copy(3, which, zz, 0, 0, me + 4).wait_send())
+            pl.when((zz >= z) & has_down)(lambda: copy(4, which, zz, 0, 0, me - 4).wait_send())
         return carry
 
     lax.fori_loop(0, line, drain, 0)
@@ -227,7 +221,7 @@
         scratch_shapes=[
             pltpu.VMEM((layer_count, train_rows, width), jnp.bfloat16),
             pltpu.VMEM((layer_count, train_rows, width), jnp.bfloat16),
-            pltpu.VMEM((2, toks, layer_count, rows, width), jnp.bfloat16),
+            pltpu.VMEM((2, layer_count, toks, rows, width), jnp.bfloat16),
             pltpu.VMEM((Q, train_rows), jnp.float32),
             pltpu.VMEM((layers - 1, q_block, train_rows), jnp.float32),
             dma((2,)),

time: 62.6 us -> 47.1 us (0.75)
  Pallas kernels: 60.5 us -> 45 us
    pallas_call x1, Pallas kernels: 60.5 us -> 45 us  [on_device(): pl.pallas_call(functools.partial(kernel, layers, line), out_shape=jax.Sha...]
where the time goes in v2:
time: 47.1 us; the launch traced here: 46.9 us
  Pallas kernels  45 us (96%)
  local copies, waits for them, and re-layouts  1.87 us (4%)
    pallas_call x1, Pallas kernels, on_device(): pl.pallas_call(functools.partial(kernel, layers, line), out_shape=jax.Sha...  45 us
    unnamed x1, local copies, waits for them, and re-layouts  1.87 us

profile of v2, /device:TPU:0, one launch (start us, length us, event | category | flops | bytes accessed | tf_op | source)
XLA Modules:
  0.0 46.9 jit_solution(16706510173226628069)
XLA Ops:
  0.0 45.0 %shard_map.55 = f32[64,2048]{1,0:T(8,128)} custom-call(bf16[2,2048,256]{2,1,0:T(8,128)(2,1)} %train_a.1, bf16[2,2048,256]{2,1,0:T(8,128)(2,1)} %train_g.1, bf16[2,128,256]{2,1,0:T(8,128)(2,1)} %test_a.1, bf16[2,128,256]{2,1,0:T(8,128)(2,1)} %test_g.1, s32[16,1,128]{2,1,0:T(1,128)} %bitcast.1), custom_call_target="tpu_custom_call" | custom-call | tf_op jit(solution)/shard_map/pallas_call | solution.py:216
  45.0 1.9 %copy.7 = f32[64,2048]{1,0:T(8,128)} copy(f32[64,2048]{1,0:T(8,128)} %shard_map.55) | data formatting | bytes 1048576

commit v3 on v2

--- a/solution.py
+++ b/solution.py
@@ -97,11 +97,23 @@
         copy(1, which, z, 0, 3, y_dev, src).start()
 
     acc[...] = jnp.zeros_like(acc)
-    tile = math.gcd(train_rows, 1024)
+    _, tiles, _, tile = xbuf.shape
     labels = lax.broadcasted_iota(jnp.int32, (Q, rows), 0)
     nt = (((1,), (1,)), ((), ()))
 
-    def accumulate(zz, first, columns):
+    def exchange(step, j):
+        to = lax.rem(core + step, layers)
+        theirs = pl.ds(pl.multiple_of(to * q_block, q_block), q_block)
+        return pltpu.make_async_remote_copy(
+            src_ref=acc.at[theirs, pl.ds(pl.multiple_of(j * tile, tile), tile)],
+            dst_ref=xbuf.at[step - 1, j],
+            send_sem=xs_sem.at[step - 1, j],
+            recv_sem=xr_sem.at[step - 1, j],
+            device_id={"layer": to},
+            device_id_type=MESH,
+        )
+
+    def accumulate(zz, first, columns, final=None):
         one_hot = [
             jnp.where(ids_ref[zz * 4 + c] == labels, 1.0, 0.0).astype(jnp.bfloat16)
             for c in columns
@@ -126,9 +138,16 @@
             acc[:, at] += jnp.dot(
                 select, jnp.concatenate(products, axis=0), preferred_element_type=jnp.float32
             )
+            if final is not None:
+
+                @pl.when(final)
+                def _():
+                    for step in range(1, layers):
+                        exchange(step, j).start()
+
             return carry
 
-        lax.fori_loop(0, train_rows // tile, one_tile, 0)
+        lax.fori_loop(0, tiles, one_tile, 0)
 
     for which, (src, dst) in enumerate(((train_a, ta), (train_g, tg))):
         pltpu.make_async_copy(src, dst, train_sem.at[which]).wait()
@@ -163,25 +182,11 @@
             zd = nth(i - 1)
             for which in range(2):
                 arrived(which, zd, 1)
-            accumulate(zd, 0, (own_col, d_col))
+            accumulate(zd, 0, (own_col, d_col), i == line)
 
         return carry
 
     lax.fori_loop(0, line + 1, stage, 0)
-
-    def exchange(step):
-        to = lax.rem(core + step, layers)
-        return pltpu.make_async_remote_copy(
-            src_ref=acc.at[pl.ds(pl.multiple_of(to * q_block, q_block), q_block)],
-            dst_ref=xbuf.at[step - 1],
-            send_sem=xs_sem.at[step - 1],
-            recv_sem=xr_sem.at[step - 1],
-            device_id={"layer": to},
-            device_id_type=MESH,
-        )
-
-    for step in range(1, layers):
-        exchange(step).start()
 
     def drain(zz, carry):
         for which in range(2):
@@ -195,20 +200,25 @@
     lax.fori_loop(0, line, drain, 0)
 
     mine = pl.ds(pl.multiple_of(core * q_block, q_block), q_block)
-    for step in range(1, layers):
-        exchange(step).wait_recv()
-    result = acc[mine, :]
-    for step in range(1, layers):
-        result = result + xbuf[step - 1]
-    out_ref[...] = result
-    for step in range(1, layers):
-        exchange(step).wait_send()
+    for j in range(tiles):
+        at = pl.ds(j * tile, tile)
+        for step in range(1, layers):
+            exchange(step, j).wait_recv()
+        result = acc[mine, at]
+        for step in range(1, layers):
+            result = result + xbuf[step - 1, j]
+        out_ref[:, at] = result
+    for j in range(tiles):
+        for step in range(1, layers):
+            exchange(step, j).wait_send()
 
 
 def on_device(layers, toks, train_act, train_grad, test_act, test_grad, segment_ids):
     layer_count, train_rows, width = train_act.shape
     rows = test_act.shape[1]
     line = toks // 4
+    tile = math.gcd(train_rows, 1024)
+    tiles = train_rows // tile
     q_block = Q // layers
     ids = segment_ids.reshape(toks, 1, rows)
     dma = pltpu.SemaphoreType.DMA
@@ -223,13 +233,13 @@
             pltpu.VMEM((layer_count, train_rows, width), jnp.bfloat16),
             pltpu.VMEM((2, layer_count, toks, rows, width), jnp.bfloat16),
             pltpu.VMEM((Q, train_rows), jnp.float32),
-            pltpu.VMEM((layers - 1, q_block, train_rows), jnp.float32),
+            pltpu.VMEM((layers - 1, tiles, q_block, tile), jnp.float32),
             dma((2,)),
             dma((2,)),
             dma((2, toks)),
             dma((5, 2, line)),
-            dma((layers - 1,)),
-            dma((layers - 1,)),
+            dma((layers - 1, tiles)),
+            dma((layers - 1, tiles)),
         ],
         compiler_params=pltpu.CompilerParams(
             collective_id=0, has_side_effects=True, vmem_limit_bytes=63 * 1024 * 1024

time: 47.1 us -> 46.7 us (level)
  no operation moved by 1% of the time
where the time goes in v3:
time: 46.7 us; the launch traced here: 46.5 us
  Pallas kernels  44.7 us (96%)
  local copies, waits for them, and re-layouts  1.87 us (4%)
    pallas_call x1, Pallas kernels, on_device(): pl.pallas_call(functools.partial(kernel, layers, line), out_shape=jax.Sha...  44.7 us
    unnamed x1, local copies, waits for them, and re-layouts  1.87 us

profile of v3, /device:TPU:0, one launch (start us, length us, event | category | flops | bytes accessed | tf_op | source)
XLA Modules:
  0.0 46.5 jit_solution(2718740003350540472)
XLA Ops:
  0.0 44.7 %shard_map.55 = f32[64,2048]{1,0:T(8,128)} custom-call(bf16[2,2048,256]{2,1,0:T(8,128)(2,1)} %train_a.1, bf16[2,2048,256]{2,1,0:T(8,128)(2,1)} %train_g.1, bf16[2,128,256]{2,1,0:T(8,128)(2,1)} %test_a.1, bf16[2,128,256]{2,1,0:T(8,128)(2,1)} %test_g.1, s32[16,1,128]{2,1,0:T(1,128)} %bitcast.1), custom_call_target="tpu_custom_call" | custom-call | tf_op jit(solution)/shard_map/pallas_call | solution.py:226
  44.7 1.9 %copy.7 = f32[64,2048]{1,0:T(8,128)} copy(f32[64,2048]{1,0:T(8,128)} %shard_map.55) | data formatting | bytes 1048576
